TPU v7x, 32 devices: a whole 2x2x4 slice. The times are simulated.
32 devices in a mesh: dp: 2 (over y), ctx: 4 (over x, core), exp: 4 (over z).
Axes of the slice: x: 2, y: 2, z: 4, core: 2. Of those that a mesh axis runs over, the one named last changes fastest.
Arguments:
- tokens: bfloat16 [4096, 2048], P(('dp', 'ctx', 'exp')), may hold values from -6 to 6
- cotangent: bfloat16 [4096, 2048], P(('dp', 'ctx', 'exp')), may hold values from -6 to 6
- expert_ids: int32 [4096, 1], P(('dp', 'ctx', 'exp')), may hold values from 0 to 7; in each aligned block of 128 rows (0 to 127, 128 to 255, ...) at most 24 rows name the same one
- router_weight: bfloat16 [2048, 8], replicated, may hold values from -0.125 to 0.125
- gate_up: bfloat16 [8, 2048, 1408], P(('dp', 'exp')), may hold values from -0.125 to 0.125
- down_weight: bfloat16 [8, 704, 2048], P(('dp', 'exp')), may hold values from -0.21875 to 0.21875
Outputs:
- moe_out: bfloat16 [4096, 2048], P(('dp', 'ctx', 'exp'))
- token_grad: bfloat16 [4096, 2048], P(('dp', 'ctx', 'exp'))
- router_grad: float32 [2048, 8], replicated
Inputs may be any that keep to these rules, and one draw needn't show every extreme that they name: `expert_ids`: each token names 1 different experts; among the 128 tokens of one device (aligned blocks of 128 rows) no expert is named more than 24 times, a bound that some block reaches.
All inputs are finite; a program needn't handle non-finite values.
Results may differ from a plain program's by a relative error of at most 0.0064.
Values may be sent and summed in bfloat16 or wider, within the bound.
A program may use at most 64 MiB of HBM per device.

v0:
```python
import jax
import jax.numpy as jnp
from jax import lax
from jax.sharding import PartitionSpec as P


def expert_rows(received, gate_up, down_weight):
    row_width = received.shape[-1] // 2
    hidden_units = down_weight.shape[1]
    flat_rows = received.reshape(-1, 2 * row_width)
    inputs = flat_rows[:, :row_width]
    upstream = flat_rows[:, row_width:]
    w_in = gate_up[0]
    w_out = down_weight[0]
    pre_act = jnp.dot(inputs, w_in, preferred_element_type=jnp.float32)
    gate_pre = pre_act[:, :hidden_units]
    up_pre = pre_act[:, hidden_units:]
    sig_gate = jax.nn.sigmoid(gate_pre)
    activated = gate_pre * sig_gate
    hidden = (activated * up_pre).astype(jnp.bfloat16)
    outputs = jnp.dot(hidden, w_out, preferred_element_type=jnp.float32).astype(jnp.bfloat16)
    back_hidden = lax.dot_general(
        upstream, w_out, (((1,), (1,)), ((), ())), preferred_element_type=jnp.float32
    )
    gate_slope = sig_gate * (1.0 + gate_pre * (1.0 - sig_gate))
    back_pre = jnp.concatenate(
        [back_hidden * up_pre * gate_slope, back_hidden * activated], axis=1
    ).astype(jnp.bfloat16)
    back_in = lax.dot_general(
        back_pre, w_in, (((1,), (1,)), ((), ())), preferred_element_type=jnp.float32
    ).astype(jnp.bfloat16)
    return jnp.concatenate([outputs, back_in], axis=1).reshape(received.shape)


def per_device(tokens, cotangent, expert_ids, router_weight, gate_up, down_weight):
    tok_count, row_width = tokens.shape
    top_count = expert_ids.shape[1]
    expert_count = router_weight.shape[1]
    capacity = min(tok_count, 3 * tok_count * top_count // (2 * expert_count))
    logits = jnp.dot(tokens, router_weight, preferred_element_type=jnp.float32)
    expert_range = jnp.arange(expert_count, dtype=jnp.int32)
    chosen = (expert_ids[:, :, None] == expert_range[None, None, :]).astype(jnp.float32)
    picked = jnp.sum(chosen * logits[:, None, :], axis=2)
    gates = jax.nn.sigmoid(picked)
    cot_float = cotangent.astype(jnp.float32)
    scaled = (gates[:, :, None] * cot_float[:, None, :]).astype(jnp.bfloat16)
    copies = tokens[:, None, :]
    payload = jnp.concatenate([copies, scaled], axis=2).reshape(
        tok_count * top_count, 2 * row_width
    )
    flat_ids = expert_ids.reshape(-1)
    one_hot = (flat_ids[:, None] == expert_range[None, :]).astype(jnp.int32)
    position = jnp.sum(jnp.cumsum(one_hot, axis=0) * one_hot, axis=1) - 1
    slot_index = flat_ids * capacity + position
    send_rows = (
        jnp.zeros((expert_count * capacity, 2 * row_width), jnp.bfloat16)
        .at[slot_index]
        .set(payload)
    )
    send_rows = send_rows.reshape(expert_count, capacity, 2 * row_width)
    result = expert_rows(
        lax.all_to_all(send_rows, ("dp", "exp"), split_axis=0, concat_axis=0, tiled=True),
        gate_up,
        down_weight,
    )
    returned = lax.all_to_all(result, ("dp", "exp"), split_axis=0, concat_axis=0, tiled=True)
    answers = returned.reshape(expert_count * capacity, 2 * row_width)[slot_index]
    answers = answers.reshape(tok_count, top_count, 2 * row_width)
    outputs = answers[:, :, :row_width].astype(jnp.float32)
    back_in = answers[:, :, row_width:].astype(jnp.float32)
    moe_out = jnp.sum(gates[:, :, None] * outputs, axis=1).astype(jnp.bfloat16)
    agreement = jnp.sum(cot_float[:, None, :] * outputs, axis=2)
    logit_grad = gates * (1.0 - gates) * agreement
    dense_grad = jnp.sum(chosen * logit_grad[:, :, None], axis=1).astype(jnp.bfloat16)
    router_back = lax.dot_general(
        dense_grad, router_weight, (((1,), (1,)), ((), ())), preferred_element_type=jnp.float32
    )
    token_grad = (jnp.sum(back_in, axis=1) + router_back).astype(jnp.bfloat16)
    total_tokens = tok_count * lax.axis_size("dp") * lax.axis_size("ctx") * lax.axis_size("exp")
    partial_grad = lax.dot_general(
        tokens, dense_grad, (((0,), (0,)), ((), ())), preferred_element_type=jnp.float32
    )
    router_grad = lax.psum(partial_grad, ("dp", "ctx", "exp")) / total_tokens
    return (moe_out, token_grad, router_grad)


def solution(mesh):
    in_specs = (
        P(("dp", "ctx", "exp"), None),
        P(("dp", "ctx", "exp"), None),
        P(("dp", "ctx", "exp"), None),
        P(),
        P(("dp", "exp"), None, None),
        P(("dp", "exp"), None, None),
    )
    out_specs = (P(("dp", "ctx", "exp"), None), P(("dp", "ctx", "exp"), None), P())
    return jax.shard_map(
        per_device, mesh=mesh, in_specs=in_specs, out_specs=out_specs, check_vma=False
    )
```

profile of v0, /device:TPU:0, one launch (start us, length us, event | category | flops | bytes accessed | tf_op | source)
XLA Modules:
  0.0 244.2 jit_solution(8978612052933089696)
XLA Ops:
  7.2 0.8 fusion.32
  8.0 0.1 copy.9
  8.1 0.2 reduce_window_sum.11
  8.3 0.7 select_reduce_fusion
  9.0 0.7 fusion.40
  9.7 1.3 fusion.15
  11.0 2.0 fusion.30
  13.0 3.8 %scatter_custom_fusion = bf16[192,4096]{1,0:T(8,128)(2,1)} fusion(s32[128]{0:T(128)S(1)} %fusion.40, bf16[128,1,2048]{2,0,1:T(8,128)(2,1)} %fusion.30, bf16[]{:T(256)} %constant.28, bf16[128,1,2048]{2,0,1:T(8,128)(2,1)S(1)} %bitcast.55, bf16[]{:T(256)} %constant.10.clone.1), kind=kCustom, calls=%fused_computation.26 | custom fusion | flops 2097152 | bytes 2621444 | tf_op jit(solution)/shard_map/scatter | solution.py:58
  16.9 45.2 %all_to_all.10 = bf16[8,24,4096]{2,1,0:T(8,128)(2,1)S(1)} all-to-all(bf16[8,24,4096]{2,1,0:T(8,128)(2,1)} %bitcast.54), channel_id=1, replica_groups=mesh['dp'=2,'ctx'=4,'exp'=4] {'dp','exp'}, dimensions={0} | all-to-all | bytes 3145728 | tf_op jit(solution)/shard_map/all_to_all | solution.py:62
  62.1 4.2 %fusion.2 = f32[192,1408]{1,0:T(8,128)S(1)} fusion(bf16[1,2048,1408]{2,1,0:T(8,128)(2,1)} %param.10, bf16[192,4096]{1,0:T(8,128)(2,1)S(1)} %bitcast.58), kind=kOutput, calls=%fused_computation.4 | convolution fusion | flops 1107296256 | bytes 7634944 | tf_op jit(solution)/shard_map/dot_general | solution.py:15
  66.3 1.1 multiply_convert_fusion.1
  67.5 0.9 fusion.8
  68.4 2.1 fusion.11
  70.4 1.3 pad_maximum_fusion
  71.7 4.3 %all-to-all-start.1 = ((bf16[8,24,4096]{2,1,0:T(8,128)(2,1)}), bf16[8,24,4096]{2,1,0:T(8,128)(2,1)}, u32[]{:S(2)}, u32[]{:S(2)}) async-start(bf16[8,24,4096]{2,1,0:T(8,128)(2,1)} %bitcast.53), calls=%async_computation.1 | async-start | bytes 3145728 | tf_op jit(solution)/shard_map/all_to_all | solution.py:66
  76.0 0.0 all-reduce.2.cloned.1.call-start
  76.1 36.9 %all-to-all-done.1 = bf16[8,24,4096]{2,1,0:T(8,128)(2,1)} async-done(((bf16[8,24,4096]{2,1,0:T(8,128)(2,1)}), bf16[8,24,4096]{2,1,0:T(8,128)(2,1)}, u32[]{:S(2)}, u32[]{:S(2)}) %all-to-all-start.1) | async-done | bytes 1572896 | tf_op jit(solution)/shard_map/all_to_all | solution.py:66
  113.0 4.8 %gather_fusion = bf16[128,4096]{1,0:T(8,128)(2,1)} fusion(bf16[192,4096]{1,0:T(8,128)(2,1)} %bitcast.11, s32[1024]{0:T(1024)S(1)} %pad_clamp_fusion), kind=kCustom, calls=%fused_computation | custom fusion | bytes 2097664 | tf_op jit(solution)/shard_map/gather | solution.py:67
  117.8 2.3 fusion.18
  120.0 0.8 convolution_bitcast_fusion
  120.8 0.0 all-reduce.2.cloned.1.call-update
  120.9 2.2 fusion.14
  123.1 112.8 %all-reduce.2.cloned.1.call-done = f32[2048,8]{0,1:T(8,128)} async-done(((f32[2048,8]{0,1:T(8,128)}), f32[2048,8]{0,1:T(8,128)}) %all-reduce.2.cloned.1.call-update) | async-done | bytes 65552 | tf_op jit(solution)/shard_map/psum | solution.py:83
  235.9 1.5 broadcast_multiply_fusion
  (17 shorter events, 0.1 us)
Async XLA Ops:
  7.2 59.1 %copy-start = (bf16[1,704,2048]{2,1,0:T(8,128)(2,1)S(1)}, bf16[1,704,2048]{2,1,0:T(8,128)(2,1)}, u32[]{:S(2)}) copy-start(bf16[1,704,2048]{2,1,0:T(8,128)(2,1)} %param.11) | copy-start | bytes 8650756
  7.2 5.9 %copy-start.1 = (bf16[128,2048]{1,0:T(8,128)(2,1)S(1)}, bf16[128,2048]{1,0:T(8,128)(2,1)}, u32[]{:S(2)}) copy-start(bf16[128,2048]{1,0:T(8,128)(2,1)} %param.6) | copy-start | bytes 1572868
  62.1 6.3 %slice-start = ((s8[5767168]{0:T(1024)(128)(4,1)}), s8[4194304]{0:T(1024)(128)(4,1)S(1)}, s32[]{:S(2)}) async-start(s8[5767168]{0:T(1024)(128)(4,1)} %bitcast.65), calls=%async_computation.3 | async-start | bytes 8388608
  66.3 2.1 slice-start.1
  71.7 41.2 %all-to-all-start.1 = ((bf16[8,24,4096]{2,1,0:T(8,128)(2,1)}), bf16[8,24,4096]{2,1,0:T(8,128)(2,1)}, u32[]{:S(2)}, u32[]{:S(2)}) async-start(bf16[8,24,4096]{2,1,0:T(8,128)(2,1)} %bitcast.53), calls=%async_computation.1 | async-start | bytes 3145728 | tf_op jit(solution)/shard_map/all_to_all | solution.py:66
  76.0 159.9 %all-reduce.2.cloned.1.call-start = ((), (), s32[]{:S(2)}) async-start(), calls=%async_computation.2 | async-start | bytes 131072 | tf_op jit(solution)/shard_map/psum | solution.py:83
  117.8 2.3 copy-start.3
  117.8 3.1 %copy-start.2 = (bf16[2048,8]{0,1:T(8,128)(2,1)S(1)}, bf16[2048,8]{0,1:T(8,128)(2,1)}, u32[]{:S(2)}) copy-start(bf16[2048,8]{0,1:T(8,128)(2,1)} %param.9) | copy-start | bytes 98308
Sparse Core Ops, SparseCore 0:
  121.0 114.8 all-reduce.1
where the time goes:
time: 246 us; the launch traced here: 244 us
  waiting for transfers between devices  150 us (61%)
  blocking collectives  45.2 us (18%)
  between operations  14.2 us (6%)
  other arithmetic  13.3 us (5%)
  matrix products  12.6 us (5%)
  local copies, waits for them, and re-layouts  4.96 us (2%)
  starting transfers between devices  4.33 us (2%)
    psum x1, waiting for transfers between devices, per_device(): router_grad = lax.psum(partial_grad, ('dp', 'ctx', 'exp')) / total_tokens  113 us
    all_to_all x1, blocking collectives, per_device(): lax.all_to_all(send_rows, ('dp', 'exp'), split_axis=0, concat_axis=0, til...  45.2 us
    all_to_all x1, waiting for transfers between devices, per_device(): lax.all_to_all(result, ('dp', 'exp'), split_axis=0, concat_axis=0, tiled=...  36.9 us
  transfers between devices with their start and end apart: 2, of which 2 were waited for; matrix products, arithmetic and copies ran while one was open for 1% of the time, Pallas kernels for 0%

commit v1 on v0

v1 whole, which is shorter than its diff:
```python
import functools

import jax
import jax.numpy as jnp
from jax import lax
from jax.experimental import pallas as pl
from jax.experimental.pallas import tpu as pltpu
from jax.sharding import PartitionSpec as P

MESH = pl.DeviceIdType.MESH
F32 = jnp.float32
BF16 = jnp.bfloat16
NT = (((1,), (1,)), ((), ()))


def plan(n_dp, n_exp):
    half = n_exp // 2
    cut = (half + 1) // 2
    far_a = [(d, 1, o) for o in range(cut) for d in range(n_dp)]
    near = [(d, 0, o) for o in range(half) for d in range(n_dp)]
    far_b = [(d, 1, o) for o in range(cut, half) for d in range(n_dp)]
    return [chunk for chunk in (far_a, near, far_b) if chunk]


def kernel(n_dp, n_ctx, n_exp, cap, total, tok, cot, ids, rw, gu_hbm, dn_hbm,
           moe_out, grad_out, rg_out,
           send, recv, res, ret, gu, dn, mine, summed, terms, columns,
           w_sem, fwd_send, fwd_recv, ret_send, ret_recv,
           ctx_send, ctx_recv, col_send, col_recv):
    me_dp, me_ctx, me_exp = lax.axis_index("dp"), lax.axis_index("ctx"), lax.axis_index("exp")
    me = me_dp * n_exp + me_exp
    half = n_exp // 2
    chunks = plan(n_dp, n_exp)
    slots = [slot for chunk in chunks for slot in chunk]
    count = len(slots)
    own = slots.index((0, 0, 0))
    tokens_here, width = tok.shape
    hidden_units = dn.shape[0]
    experts = rw.shape[1]
    rows = 2 * cap

    def peer(slot, way):
        d, h, o = slot
        if way < 0:
            d, h, o = (n_dp - d) % n_dp, h, (half - o) % half
        to_dp = lax.rem(me_dp + d, n_dp)
        to_half = lax.rem(me_exp // half + h, 2)
        to_low = lax.rem(lax.rem(me_exp, half) + o, half)
        return to_dp, to_half * half + to_low

    def at(pair):
        return {"dp": pair[0], "ctx": me_ctx, "exp": pair[1]}

    def at_ctx(j):
        return {"dp": me_dp, "ctx": j, "exp": me_exp}

    gu_copy = pltpu.make_async_copy(gu_hbm.at[0], gu, w_sem.at[0])
    dn_copy = pltpu.make_async_copy(dn_hbm.at[0], dn, w_sem.at[1])
    gu_copy.start()
    dn_copy.start()

    barrier = pltpu.get_barrier_semaphore()
    for k, slot in enumerate(slots):
        if k != own:
            pl.semaphore_signal(barrier, inc=1, device_id=at(peer(slot, 1)), device_id_type=MESH)
    for j in range(1, n_ctx):
        pl.semaphore_signal(
            barrier, inc=1, device_id=at_ctx(lax.rem(me_ctx + j, n_ctx)), device_id_type=MESH
        )

    ids_col = jnp.broadcast_to(ids[...], (tokens_here, tokens_here))
    r_iota = lax.broadcasted_iota(jnp.int32, (tokens_here, tokens_here), 0)
    c_iota = lax.broadcasted_iota(jnp.int32, (tokens_here, tokens_here), 1)
    ids_row = jnp.sum(jnp.where(r_iota == c_iota, ids_col, 0), axis=0, keepdims=True)
    same = ids_col == ids_row
    place_row = jnp.sum(jnp.where(same & (r_iota < c_iota), 1, 0), axis=0, keepdims=True)
    place_col = jnp.sum(jnp.where(same & (c_iota < r_iota), 1, 0), axis=1, keepdims=True)
    for k, slot in enumerate(slots):
        to_dp, to_exp = peer(slot, 1)
        expert = to_dp * n_exp + to_exp
        place_row = place_row + jnp.where(ids_row == expert, k * rows, 0)
        place_col = place_col + jnp.where(ids[...] == expert, k * rows, 0)

    pick_iota = lax.broadcasted_iota(jnp.int32, (count * rows, tokens_here), 0)
    pick_tok = jnp.where(pick_iota == place_row, 1.0, 0.0).astype(BF16)
    pick_cot = jnp.where(pick_iota == place_row + cap, 1.0, 0.0).astype(BF16)
    pick = jnp.concatenate([pick_tok, pick_cot], axis=1)
    stacked = jnp.concatenate([tok[...], cot[...]], axis=0)

    fwd = []
    back = []
    for k, slot in enumerate(slots):
        if k == own:
            fwd.append(None)
            back.append(None)
            continue
        fwd.append(
            pltpu.make_async_remote_copy(
                src_ref=send.at[k], dst_ref=recv.at[k],
                send_sem=fwd_send.at[k], recv_sem=fwd_recv.at[k],
                device_id=at(peer(slot, 1)), device_id_type=MESH,
            )
        )
        back.append(
            pltpu.make_async_remote_copy(
                src_ref=res.at[k], dst_ref=ret.at[k],
                send_sem=ret_send.at[k], recv_sem=ret_recv.at[k],
                device_id=at(peer(slot, -1)), device_id_type=MESH,
            )
        )

    first = 0
    for number, chunk in enumerate(chunks):
        last = first + len(chunk)
        packed = jnp.dot(
            pick[first * rows:last * rows], stacked, preferred_element_type=F32
        ).astype(BF16)
        send[first:last] = packed.reshape(len(chunk), rows, width)
        if number == 0:
            pl.semaphore_wait(barrier, count - 1 + n_ctx - 1)
        for k in range(first, last):
            if k != own:
                fwd[k].start()
        first = last

    lane_e = lax.broadcasted_iota(jnp.int32, (8, experts), 1)
    choose = jnp.where(lane_e == me, 1.0, 0.0).astype(BF16)
    router_row = lax.dot_general(choose, rw[...], NT, preferred_element_type=F32)[:1]

    gu_copy.wait()
    dn_copy.wait()

    router_sum = jnp.zeros((1, width), F32)
    first = 0
    for chunk in chunks:
        last = first + len(chunk)
        xs, cs = [], []
        for k in range(first, last):
            if k == own:
                block = send[k].astype(F32)
            else:
                fwd[k].wait_recv()
                block = recv[k].astype(F32)
            xs.append(block[:cap])
            cs.append(block[cap:])
        x_wide = jnp.concatenate(xs, axis=0)
        c_wide = jnp.concatenate(cs, axis=0)
        m = x_wide.shape[0]
        x = x_wide.astype(BF16)
        logits = jnp.dot(x, rw[...], preferred_element_type=F32)
        lane = lax.broadcasted_iota(jnp.int32, (m, experts), 1)
        gate = jax.nn.sigmoid(jnp.sum(jnp.where(lane == me, logits, 0.0), axis=1, keepdims=True))
        upstream = (gate * c_wide).astype(BF16)
        pre = jnp.dot(x, gu[...], preferred_element_type=F32)
        a = pre[:, :hidden_units]
        u = pre[:, hidden_units:]
        s = jax.nn.sigmoid(a)
        act = a * s
        hidden = (act * u).astype(BF16)
        out = jnp.dot(hidden, dn[...], preferred_element_type=F32).astype(BF16).astype(F32)
        back_hidden = lax.dot_general(upstream, dn[...], NT, preferred_element_type=F32)
        back_pre = jnp.concatenate(
            [back_hidden * u * (s * (1.0 + a * (1.0 - s))), back_hidden * act], axis=1
        ).astype(BF16)
        back_in = lax.dot_general(back_pre, gu[...], NT, preferred_element_type=F32)
        agreement = jnp.sum(c_wide * out, axis=1, keepdims=True)
        dense = (gate * (1.0 - gate) * agreement).astype(BF16).astype(F32)
        moe = gate * out
        grad = back_in.astype(BF16).astype(F32) + dense * router_row
        for i, k in enumerate(range(first, last)):
            part = slice(i * cap, (i + 1) * cap)
            block = jnp.concatenate([moe[part], grad[part]], axis=0).astype(BF16)
            if k == own:
                ret[k] = block
            else:
                res[k] = block
                back[k].start()
        router_sum = router_sum + jnp.sum(dense * x_wide, axis=0, keepdims=True)
        first = last

    router_sum = router_sum * (1.0 / total)
    lanes = width // mine.shape[0]
    for i in range(mine.shape[0]):
        mine[i:i + 1, :] = router_sum[:, i * lanes:(i + 1) * lanes]
    terms[me_ctx] = mine[...]
    ctx_copies = []
    for j in range(1, n_ctx):
        copy = pltpu.make_async_remote_copy(
            src_ref=mine, dst_ref=terms.at[me_ctx],
            send_sem=ctx_send.at[j], recv_sem=ctx_recv.at[me_ctx],
            device_id=at_ctx(lax.rem(me_ctx + j, n_ctx)), device_id_type=MESH,
        )
        copy.start()
        ctx_copies.append(copy)
    for j in range(1, n_ctx):
        source = lax.rem(me_ctx + j, n_ctx)
        pltpu.make_async_remote_copy(
            src_ref=mine, dst_ref=terms.at[source],
            send_sem=ctx_send.at[j], recv_sem=ctx_recv.at[source],
            device_id=at_ctx(source), device_id_type=MESH,
        ).wait_recv()
    column = terms[0]
    for j in range(1, n_ctx):
        column = column + terms[j]
    summed[...] = column
    columns[me] = column
    col_copies = []
    for k, slot in enumerate(slots):
        if k != own:
            copy = pltpu.make_async_remote_copy(
                src_ref=summed, dst_ref=columns.at[me],
                send_sem=col_send.at[k], recv_sem=col_recv.at[me],
                device_id=at(peer(slot, 1)), device_id_type=MESH,
            )
            copy.start()
            col_copies.append(copy)

    spot_iota = lax.broadcasted_iota(jnp.int32, (tokens_here, count * rows), 1)
    put_moe = jnp.where(spot_iota == place_col, 1.0, 0.0).astype(BF16)
    put_grad = jnp.where(spot_iota == place_col + cap, 1.0, 0.0).astype(BF16)
    put = jnp.concatenate([put_moe, put_grad], axis=0)
    split = count - len(chunks[-1])
    for first, last in ((0, split), (split, count)):
        for k in range(first, last):
            if k != own:
                back[k].wait_recv()
        came = ret[first:last].reshape((last - first) * rows, width)
        placed = jnp.dot(put[:, first * rows:last * rows], came, preferred_element_type=F32)
        if first == 0:
            moe_out[...] = placed[:tokens_here].astype(BF16)
            grad_out[...] = placed[tokens_here:].astype(BF16)
        else:
            moe_out[...] = (moe_out[...].astype(F32) + placed[:tokens_here]).astype(BF16)
            grad_out[...] = (grad_out[...].astype(F32) + placed[tokens_here:]).astype(BF16)

    for k, slot in enumerate(slots):
        if k != own:
            from_dp, from_exp = peer(slot, -1)
            source = from_dp * n_exp + from_exp
            pltpu.make_async_remote_copy(
                src_ref=summed, dst_ref=columns.at[source],
                send_sem=col_send.at[k], recv_sem=col_recv.at[source],
                device_id=at(peer(slot, -1)), device_id_type=MESH,
            ).wait_recv()
    rg_out[...] = columns[...]
    for k in range(count):
        if k != own:
            fwd[k].wait_send()
            back[k].wait_send()
    for copy in ctx_copies + col_copies:
        copy.wait_send()


def per_device(n_dp, n_ctx, n_exp, tokens, cotangent, expert_ids, router_weight, gate_up, down_weight):
    tok_count, width = tokens.shape
    experts = router_weight.shape[1]
    hidden_units = down_weight.shape[1]
    most = min(tok_count, 3 * tok_count * expert_ids.shape[1] // (2 * experts))
    cap = -(-most // 8) * 8
    count = n_dp * n_exp
    rows = 2 * cap
    total = tok_count * n_dp * n_ctx * n_exp
    lines = width // 128
    vmem = pl.BlockSpec(memory_space=pltpu.VMEM)
    hbm = pl.BlockSpec(memory_space=pl.ANY)
    dma = pltpu.SemaphoreType.DMA
    flops = 2 * 2 * count * cap * width * 3 * hidden_units
    moe, grad, columns = pl.pallas_call(
        functools.partial(kernel, n_dp, n_ctx, n_exp, cap, total),
        out_shape=(
            jax.ShapeDtypeStruct((tok_count, width), BF16),
            jax.ShapeDtypeStruct((tok_count, width), BF16),
            jax.ShapeDtypeStruct((experts, lines, 128), F32),
        ),
        in_specs=[vmem, vmem, vmem, vmem, hbm, hbm],
        out_specs=(vmem, vmem, vmem),
        scratch_shapes=[
            pltpu.VMEM((count, rows, width), BF16),
            pltpu.VMEM((count, rows, width), BF16),
            pltpu.VMEM((count, rows, width), BF16),
            pltpu.VMEM((count, rows, width), BF16),
            pltpu.VMEM((width, 2 * hidden_units), BF16),
            pltpu.VMEM((hidden_units, width), BF16),
            pltpu.VMEM((lines, 128), F32),
            pltpu.VMEM((lines, 128), F32),
            pltpu.VMEM((n_ctx, lines, 128), F32),
            pltpu.VMEM((experts, lines, 128), F32),
            dma((2,)),
            dma((count,)),
            dma((count,)),
            dma((count,)),
            dma((count,)),
            dma((n_ctx,)),
            dma((n_ctx,)),
            dma((count,)),
            dma((count,)),
        ],
        compiler_params=pltpu.CompilerParams(
            collective_id=0, has_side_effects=True, vmem_limit_bytes=58 * 1024 * 1024
        ),
        cost_estimate=pl.CostEstimate(
            flops=flops, bytes_accessed=12 * 1024 * 1024, transcendentals=0
        ),
    )(tokens, cotangent, expert_ids, router_weight, gate_up, down_weight)
    return moe, grad, columns.reshape(experts, width).T


def solution(mesh):
    in_specs = (
        P(("dp", "ctx", "exp"), None),
        P(("dp", "ctx", "exp"), None),
        P(("dp", "ctx", "exp"), None),
        P(),
        P(("dp", "exp"), None, None),
        P(("dp", "exp"), None, None),
    )
    out_specs = (P(("dp", "ctx", "exp"), None), P(("dp", "ctx", "exp"), None), P())
    shape = mesh.shape
    return jax.shard_map(
        functools.partial(per_device, shape["dp"], shape["ctx"], shape["exp"]),
        mesh=mesh, in_specs=in_specs, out_specs=out_specs, check_vma=False,
    )
```

time: 246 us -> 90.3 us (0.37)
  waiting for transfers between devices: 150 us -> 0 us
  Pallas kernels: 0 us -> 80.9 us
  blocking collectives: 45.2 us -> 0 us
  between operations: 14.2 us -> 0.64 us
  other arithmetic: 13.3 us -> 0 us
  matrix products: 12.6 us -> 0 us
  starting transfers between devices: 4.33 us -> 0 us
  local copies, waits for them, and re-layouts: 4.96 us -> 8.4 us
    psum x1 -> x0, waiting for transfers between devices: 113 us -> none  [per_device(): router_grad = lax.psum(partial_grad, ('dp', 'ctx', 'exp')) / total_tokens]
    pallas_call x0 -> x1, Pallas kernels: none -> 80.9 us  [per_device(): pl.pallas_call(functools.partial(kernel, n_dp, n_ctx, n_exp, cap, total),...]
    all_to_all x1 -> x0, blocking collectives: 45.2 us -> none  [per_device(): lax.all_to_all(send_rows, ('dp', 'exp'), split_axis=0, concat_axis=0, til...]
    all_to_all x1 -> x0, waiting for transfers between devices: 36.9 us -> none  [per_device(): lax.all_to_all(result, ('dp', 'exp'), split_axis=0, concat_axis=0, tiled=...]
    dot_general x7 -> x0, matrix products: 12.6 us -> none  [the longest x1 4.22 us: expert_rows(): pre_act = jnp.dot(inputs, w_in, preferred_element_type=jnp.float32)]
    unnamed x12 -> x5, local copies, waits for them, and re-layouts: 0.03 us -> 8.4 us
    gather x1 -> x0, local copies, waits for them, and re-layouts: 4.78 us -> none  [per_device(): returned.reshape(expert_count * capacity, 2 * row_width)[slot_index]]
    all_to_all x1 -> x0, starting transfers between devices: 4.29 us -> none  [per_device(): lax.all_to_all(result, ('dp', 'exp'), split_axis=0, concat_axis=0, tiled=...]
  transfers between devices with their start and end apart: 2 -> 0, of which waited for: 2 -> 0; matrix products, arithmetic and copies ran while one was open for 1% -> 0% of each run, Pallas kernels for 0% -> 0%
where the time goes in v1:
time: 90.3 us; the launch traced here: 89.9 us
  Pallas kernels  80.9 us (90%)
  local copies, waits for them, and re-layouts  8.4 us (9%)
    pallas_call x1, Pallas kernels, per_device(): pl.pallas_call(functools.partial(kernel, n_dp, n_ctx, n_exp, cap, total),...  80.9 us
    unnamed x5, local copies, waits for them, and re-layouts  8.4 us

profile of v1, /device:TPU:0, one launch (start us, length us, event | category | flops | bytes accessed | tf_op | source)
XLA Modules:
  0.0 89.9 jit_solution(10506385792941374225)
XLA Ops:
  0.6 1.4 %copy.9.ids = s32[128,1]{1,0:T(8,128)} copy(s32[128,1]{0,1:T(1,128)} %param.8) | data formatting | bytes 1024 | tf_op args[2]
  2.0 1.8 %copy.10.rw = bf16[2048,8]{1,0:T(8,128)(2,1)} copy(bf16[2048,8]{0,1:T(8,128)(2,1)} %param.9) | data formatting | bytes 65536 | tf_op args[3]
  3.8 80.9 %shard_map.85 = (bf16[128,2048]{1,0:T(8,128)(2,1)}, bf16[128,2048]{1,0:T(8,128)(2,1)}, f32[8,16,128]{2,1,0:T(8,128)}) custom-call(bf16[128,2048]{1,0:T(8,128)(2,1)} %tok.1, bf16[128,2048]{1,0:T(8,128)(2,1)} %cot.1, s32[128,1]{1,0:T(8,128)} %copy.9.ids, bf16[2048,8]{1,0:T(8,128)(2,1)} %copy.10.rw, bf16[1,2048,1408]{2,1,0:T(8,128)(2,1)} %gu_hbm.1, ...), custom_call_target="tpu_custom_call" | custom-call | flops 3321888768 | bytes 12582912 | tf_op jit(solution)/shard_map/pallas_call | solution.py:268
  84.7 1.5 %copy.13 = f32[1,8,16,128]{3,1,2,0:T(8,128)} copy(f32[1,8,16,128]{3,2,1,0:T(8,128)} %bitcast.8) | data formatting | bytes 131072
  86.2 1.9 %copy.16 = bf16[128,2048]{1,0:T(8,128)(2,1)} copy(bf16[128,2048]{1,0:T(8,128)(2,1)} %get-tuple-element.12) | data formatting | bytes 1048576
  88.0 1.9 %copy.17 = bf16[128,2048]{1,0:T(8,128)(2,1)} copy(bf16[128,2048]{1,0:T(8,128)(2,1)} %get-tuple-element.13) | data formatting | bytes 1048576

commit v2 on v1

--- a/solution.py
+++ b/solution.py
@@ -36,7 +36,7 @@
     own = slots.index((0, 0, 0))
     tokens_here, width = tok.shape
     hidden_units = dn.shape[0]
-    experts = rw.shape[1]
+    experts = rw.shape[0]
     rows = 2 * cap
 
     def peer(slot, way):
@@ -68,10 +68,11 @@
             barrier, inc=1, device_id=at_ctx(lax.rem(me_ctx + j, n_ctx)), device_id_type=MESH
         )
 
-    ids_col = jnp.broadcast_to(ids[...], (tokens_here, tokens_here))
+    ids_row = ids[...]
     r_iota = lax.broadcasted_iota(jnp.int32, (tokens_here, tokens_here), 0)
     c_iota = lax.broadcasted_iota(jnp.int32, (tokens_here, tokens_here), 1)
-    ids_row = jnp.sum(jnp.where(r_iota == c_iota, ids_col, 0), axis=0, keepdims=True)
+    ids_wide = jnp.broadcast_to(ids_row, (tokens_here, tokens_here))
+    ids_col = jnp.sum(jnp.where(r_iota == c_iota, ids_wide, 0), axis=1, keepdims=True)
     same = ids_col == ids_row
     place_row = jnp.sum(jnp.where(same & (r_iota < c_iota), 1, 0), axis=0, keepdims=True)
     place_col = jnp.sum(jnp.where(same & (c_iota < r_iota), 1, 0), axis=1, keepdims=True)
@@ -79,7 +80,7 @@
         to_dp, to_exp = peer(slot, 1)
         expert = to_dp * n_exp + to_exp
         place_row = place_row + jnp.where(ids_row == expert, k * rows, 0)
-        place_col = place_col + jnp.where(ids[...] == expert, k * rows, 0)
+        place_col = place_col + jnp.where(ids_col == expert, k * rows, 0)
 
     pick_iota = lax.broadcasted_iota(jnp.int32, (count * rows, tokens_here), 0)
     pick_tok = jnp.where(pick_iota == place_row, 1.0, 0.0).astype(BF16)
@@ -109,8 +110,10 @@
             )
         )
 
-    first = 0
-    for number, chunk in enumerate(chunks):
+    starts = [sum(len(c) for c in chunks[:i]) for i in range(len(chunks))]
+    order = sorted(range(len(chunks)), key=lambda i: chunks[i][0][1] == 0)
+    for number, which in enumerate(order):
+        chunk, first = chunks[which], starts[which]
         last = first + len(chunk)
         packed = jnp.dot(
             pick[first * rows:last * rows], stacked, preferred_element_type=F32
@@ -121,11 +124,9 @@
         for k in range(first, last):
             if k != own:
                 fwd[k].start()
-        first = last
-
-    lane_e = lax.broadcasted_iota(jnp.int32, (8, experts), 1)
-    choose = jnp.where(lane_e == me, 1.0, 0.0).astype(BF16)
-    router_row = lax.dot_general(choose, rw[...], NT, preferred_element_type=F32)[:1]
+
+    row_e = lax.broadcasted_iota(jnp.int32, (experts, width), 0)
+    router_row = jnp.sum(jnp.where(row_e == me, rw[...].astype(F32), 0.0), axis=0, keepdims=True)
 
     gu_copy.wait()
     dn_copy.wait()
@@ -147,7 +148,7 @@
         c_wide = jnp.concatenate(cs, axis=0)
         m = x_wide.shape[0]
         x = x_wide.astype(BF16)
-        logits = jnp.dot(x, rw[...], preferred_element_type=F32)
+        logits = lax.dot_general(x, rw[...], NT, preferred_element_type=F32)
         lane = lax.broadcasted_iota(jnp.int32, (m, experts), 1)
         gate = jax.nn.sigmoid(jnp.sum(jnp.where(lane == me, logits, 0.0), axis=1, keepdims=True))
         upstream = (gate * c_wide).astype(BF16)
@@ -242,13 +243,34 @@
                 send_sem=col_send.at[k], recv_sem=col_recv.at[source],
                 device_id=at(peer(slot, -1)), device_id_type=MESH,
             ).wait_recv()
-    rg_out[...] = columns[...]
+    for i in range(mine.shape[0]):
+        rg_out[:, i * lanes:(i + 1) * lanes] = columns[:, i, :]
     for k in range(count):
         if k != own:
             fwd[k].wait_send()
             back[k].wait_send()
     for copy in ctx_copies + col_copies:
         copy.wait_send()
+
+
+def hand_over(moe, grad, columns, moe_out, grad_out, rg_out, moe_buf, grad_buf, rg_buf, in_sem, out_sem):
+    half = moe.shape[0] // 2
+    parts = [(columns, rg_buf, rg_out)]
+    for source, buffer, target in ((moe, moe_buf, moe_out), (grad, grad_buf, grad_out)):
+        for start in (0, half):
+            cut = pl.ds(start, half)
+            parts.append((source.at[cut], buffer.at[cut], target.at[cut]))
+    loads, stores = [], []
+    for i, (source, buffer, target) in enumerate(parts):
+        loads.append(pltpu.make_async_copy(source, buffer, in_sem.at[i]))
+        stores.append(pltpu.make_async_copy(buffer, target, out_sem.at[i]))
+    for load in loads:
+        load.start()
+    for load, store in zip(loads, stores):
+        load.wait()
+        store.start()
+    for store in stores:
+        store.wait()
 
 
 def per_device(n_dp, n_ctx, n_exp, tokens, cotangent, expert_ids, router_weight, gate_up, down_weight):
@@ -270,7 +292,7 @@
         out_shape=(
             jax.ShapeDtypeStruct((tok_count, width), BF16),
             jax.ShapeDtypeStruct((tok_count, width), BF16),
-            jax.ShapeDtypeStruct((experts, lines, 128), F32),
+            jax.ShapeDtypeStruct((experts, width), F32),
         ),
         in_specs=[vmem, vmem, vmem, vmem, hbm, hbm],
         out_specs=(vmem, vmem, vmem),
@@ -301,8 +323,21 @@
         cost_estimate=pl.CostEstimate(
             flops=flops, bytes_accessed=12 * 1024 * 1024, transcendentals=0
         ),
-    )(tokens, cotangent, expert_ids, router_weight, gate_up, down_weight)
-    return moe, grad, columns.reshape(experts, width).T
+    )(tokens, cotangent, expert_ids.reshape(1, tok_count), router_weight.T, gate_up, down_weight)
+    moe, grad, columns = pl.pallas_call(
+        hand_over,
+        out_shape=tuple(jax.ShapeDtypeStruct(v.shape, v.dtype) for v in (moe, grad, columns)),
+        in_specs=[hbm, hbm, hbm],
+        out_specs=(hbm, hbm, hbm),
+        scratch_shapes=[
+            pltpu.VMEM(moe.shape, BF16),
+            pltpu.VMEM(grad.shape, BF16),
+            pltpu.VMEM(columns.shape, F32),
+            dma((5,)),
+            dma((5,)),
+        ],
+    )(moe, grad, columns)
+    return moe, grad, columns.T
 
 
 def solution(mesh):

time: 90.3 us -> 81.9 us (0.907)
  local copies, waits for them, and re-layouts: 8.4 us -> 0 us
    unnamed x5 -> x0, local copies, waits for them, and re-layouts: 8.4 us -> none
    pallas_call x0 -> x1, Pallas kernels: none -> 2.04 us  [per_device(): pl.pallas_call(hand_over, out_shape=tuple((jax.ShapeDtypeStruct(v.shape,...]
    pallas_call x1, Pallas kernels: 80.9 us -> 79.1 us  [per_device(): pl.pallas_call(functools.partial(kernel, n_dp, n_ctx, n_exp, cap, total),...]
where the time goes in v2:
time: 81.9 us; the launch traced here: 81.8 us
  Pallas kernels  81.1 us (99%)
    pallas_call x1, Pallas kernels, per_device(): pl.pallas_call(functools.partial(kernel, n_dp, n_ctx, n_exp, cap, total),...  79.1 us
    pallas_call x1, Pallas kernels, per_device(): pl.pallas_call(hand_over, out_shape=tuple((jax.ShapeDtypeStruct(v.shape,...  2.04 us

profile of v2, /device:TPU:0, one launch (start us, length us, event | category | flops | bytes accessed | tf_op | source)
XLA Modules:
  0.0 81.8 jit_solution(14724591447493730911)
XLA Ops:
  0.6 79.1 %shard_map.85 = (bf16[128,2048]{1,0:T(8,128)(2,1)}, bf16[128,2048]{1,0:T(8,128)(2,1)}, f32[8,2048]{1,0:T(8,128)}) custom-call(bf16[128,2048]{1,0:T(8,128)(2,1)} %tok.1, bf16[128,2048]{1,0:T(8,128)(2,1)} %cot.1, s32[1,128]{1,0:T(1,128)} %bitcast.5, bf16[8,2048]{1,0:T(8,128)(2,1)} %bitcast.4, bf16[1,2048,1408]{2,1,0:T(8,128)(2,1)} %gu_hbm.1, ...), custom_call_target="tpu_custom_call" | custom-call | flops 3321888768 | bytes 12582912 | tf_op jit(solution)/shard_map/pallas_call | solution.py:290
  79.7 2.0 %shard_map.86 = (bf16[128,2048]{1,0:T(8,128)(2,1)}, bf16[128,2048]{1,0:T(8,128)(2,1)}, f32[8,2048]{1,0:T(8,128)}) custom-call(bf16[128,2048]{1,0:T(8,128)(2,1)} %get-tuple-element.9.moe, bf16[128,2048]{1,0:T(8,128)(2,1)} %get-tuple-element.10.grad, f32[8,2048]{1,0:T(8,128)} %get-tuple-element.11.columns), custom_call_target="tpu_custom_call" | custom-call | tf_op jit(solution)/shard_map/pallas_call | solution.py:327
